TPU v7x, 256 devices: a whole 4x4x8 slice. The times are simulated.
256 devices in a mesh: video: 8 (over x, y_hi), context: 32 (over y_lo, z, core).
Axes of the slice: x: 4, y: 4 (y_hi: 2, y_lo: 2; y = y_hi * 2 + y_lo), z: 8, core: 2. Of those that a mesh axis runs over, the one named last changes fastest.
Arguments:
- queries: bfloat16 [32768, 4096], P(('video', 'context')), parts along dimension 0, may hold values from -135 to 135
- keys: bfloat16 [32768, 4096], P(('video', 'context')), parts along dimension 0, may hold values from -5 to 5
- values: bfloat16 [32768, 4096], P(('video', 'context')), parts along dimension 0, may hold values from -6 to 6
- value_layer_input: bfloat16 [32768, 4096], P(('video', 'context')), parts along dimension 0, may hold values from -6 to 6
- adapter_down_weight: bfloat16 [4096, 64], replicated, may hold values from -0.09375 to 0.09375
- adapter_up_weight: bfloat16 [4096, 64], replicated, may hold values from -0.75 to 0.75
- neighbors: int32 [512, 4], P(('video', 'context')), parts along dimension 0, may hold values from 0 to 63, as said below
Outputs:
- student_out: bfloat16 [32768, 4096], P(('video', 'context')), parts along dimension 0
- grad_down: float32 [32768, 64], P(('video', 'context')), parts along dimension 0
- grad_up: float32 [32768, 64], P(('video', 'context')), parts along dimension 0
There are 8 independent parts, one for each index of `video`. A program takes and returns all parts, laid end to end along the dimension named above; an argument that names none is the same for every part. Nothing has to cross between parts.
Inputs may be any that keep to these rules, and one draw needn't show every extreme that they name: `neighbors`: row i begins with i itself; its 4 entries are distinct tiles of the slab of tile i, the slab before or the slab after, where slab = tile // 2.
All inputs are finite; a program needn't handle non-finite values.
Results may differ from a plain program's by a relative error of at most 0.008.
Values may be sent and summed in bfloat16 or wider, within the bound.
A program may use at most 64 MiB of HBM per device.

v0:
```python
import jax
import jax.numpy as jnp
from jax import lax
from jax.sharding import PartitionSpec as P

H = 32


def padded(block, sides, width):
    for axis, dim in sides:
        count = lax.axis_size(axis)
        forward = [(i, i + 1) for i in range(count - 1)]
        backward = [(target, source) for source, target in forward]
        low = lax.ppermute(
            lax.slice_in_dim(block, block.shape[dim] - width, None, axis=dim), axis, forward
        )
        high = lax.ppermute(lax.slice_in_dim(block, 0, width, axis=dim), axis, backward)
        block = jnp.concatenate([low, block, high], axis=dim)
    return block


def shifted(block, axis, distance):
    devices = range(lax.axis_size(axis))
    route = [(i - distance, i) for i in devices if i - distance in devices]
    return lax.ppermute(block, axis, route)


def teacher_heads(pieces):
    queries, keys, values = pieces
    total = queries.shape[0]
    heads = queries.shape[2]
    width = queries.shape[3]
    queries = queries.reshape(total, heads, width)
    keys = keys.reshape(total, heads, width)
    values = values.reshape(total, heads, width)
    block = min(512, total)
    scale = width ** (-0.5)

    def one_block(query_block):
        scores = (
            jnp.einsum("qhd,khd->hqk", query_block, keys, preferred_element_type=jnp.float32)
            * scale
        )
        top = jnp.max(scores, axis=2, keepdims=True)
        expo = jnp.exp(scores - top)
        weights = (expo / jnp.sum(expo, axis=2, keepdims=True)).astype(jnp.bfloat16)
        return jnp.einsum(
            "hqk,khd->qhd", weights, values, preferred_element_type=jnp.float32
        ).astype(jnp.bfloat16)

    outputs = lax.map(one_block, queries.reshape(total // block, block, heads, width))
    return outputs.reshape(total, 1, heads, width)


def contract_rows(left, right):
    return lax.dot_general(
        left,
        right,
        (((0,), (0,)), ((), ())),
        precision=lax.Precision.HIGHEST,
        preferred_element_type=jnp.float32,
    )


def local(
    queries, keys, values, value_layer_input, adapter_down_weight, adapter_up_weight, neighbors
):
    tok = queries.shape[0]
    width = queries.shape[1]
    adapter_rank = adapter_down_weight.shape[1]
    groups = lax.axis_size("context")
    head_size = width // H
    per_group = H // groups

    def split_heads(array):
        return array.reshape(tok, groups, per_group, head_size)

    teacher = teacher_heads(
        (
            lax.all_to_all(
                split_heads(queries), "context", split_axis=1, concat_axis=0, tiled=True
            ),
            lax.all_to_all(split_heads(keys), "context", split_axis=1, concat_axis=0, tiled=True),
            lax.all_to_all(split_heads(values), "context", split_axis=1, concat_axis=0, tiled=True),
        )
    )
    teacher = lax.all_to_all(teacher, "context", split_axis=0, concat_axis=1, tiled=True).reshape(
        tok, width
    )
    adapter_down_rows = jnp.dot(
        value_layer_input, adapter_down_weight, preferred_element_type=jnp.float32
    ).astype(jnp.bfloat16)
    adapter_value_term = lax.dot_general(
        adapter_down_rows,
        adapter_up_weight,
        (((1,), (1,)), ((), ())),
        preferred_element_type=jnp.float32,
    )
    learner_values = (values.astype(jnp.float32) + adapter_value_term).astype(jnp.bfloat16)
    up_float = adapter_up_weight.astype(jnp.float32)
    window = padded(jnp.stack([keys, learner_values]), (("context", 1),), tok)
    window_keys = window[0].reshape(3 * tok, H, head_size)
    window_values = window[1].reshape(3 * tok, H, head_size)
    tile_count = neighbors.shape[0]
    tile = tok // tile_count
    slab = lax.axis_index("context")
    offsets = neighbors - (slab - 1) * tile_count
    slots = jnp.arange(3 * tile_count, dtype=jnp.int32)
    tile_mask = jnp.any(offsets[:, :, None] == slots[None, None, :], axis=1)
    token_mask = jnp.broadcast_to(
        tile_mask[:, None, :, None], (tile_count, tile, 3 * tile_count, tile)
    ).reshape(tok, 3 * tok)
    scale = head_size ** (-0.5)
    scores = (
        jnp.einsum(
            "qhd,khd->hqk",
            queries.reshape(tok, H, head_size),
            window_keys,
            preferred_element_type=jnp.float32,
        )
        * scale
    )
    scores = jnp.where(token_mask[None], scores, -1e30)
    top = jnp.max(scores, axis=2, keepdims=True)
    expo = jnp.exp(scores - top)
    weights = (expo / jnp.sum(expo, axis=2, keepdims=True)).astype(jnp.bfloat16)
    student = jnp.einsum(
        "hqk,khd->qhd", weights, window_values, preferred_element_type=jnp.float32
    ).reshape(tok, width)
    student_out = student.astype(jnp.bfloat16)
    factor = (tok * groups) ** (-0.5)
    output_grad = ((student - teacher.astype(jnp.float32)) * factor).astype(jnp.bfloat16)
    window_grad = jnp.einsum(
        "hqk,qhd->khd",
        weights,
        output_grad.reshape(tok, H, head_size),
        preferred_element_type=jnp.float32,
    )
    window_grad = window_grad.reshape(3 * tok, width)
    from_above = shifted(window_grad[:tok], "context", -1)
    from_below = shifted(window_grad[2 * tok :], "context", 1)
    grad_pieces = [window_grad[tok : 2 * tok], from_above, from_below]
    input_float = value_layer_input.astype(jnp.float32)
    down_float = adapter_down_rows.astype(jnp.float32)
    input_pieces = [input_float, input_float, input_float]
    down_segments = [down_float, down_float, down_float]
    hidden_pieces = [
        jnp.dot(
            segment, up_float, precision=lax.Precision.HIGHEST, preferred_element_type=jnp.float32
        )
        for segment in grad_pieces
    ]
    summed = jnp.zeros((width // groups * lax.axis_size("context"), 2 * adapter_rank), jnp.float32)
    for inputs, hidden, grads, downs in zip(
        input_pieces, hidden_pieces, grad_pieces, down_segments
    ):
        summed = summed + jnp.concatenate(
            [contract_rows(inputs, hidden), contract_rows(grads, downs)], axis=1
        )
    adapter = lax.psum_scatter(summed, "context", scatter_dimension=0, tiled=True)
    return (student_out, adapter[:, :adapter_rank], adapter[:, adapter_rank:])


def solution(mesh):
    placed = (
        P(("video", "context"), None),
        P(("video", "context"), None),
        P(("video", "context"), None),
        P(("video", "context"), None),
        P(),
        P(),
        P(("video", "context"), None),
    )
    return jax.shard_map(
        local,
        mesh=mesh,
        in_specs=placed,
        out_specs=(
            P(("video", "context"), None),
            P(("video", "context"), None),
            P(("video", "context"), None),
        ),
        check_vma=False,
    )
```

profile of v0, /device:TPU:1, one launch (start us, length us, event | category | flops | bytes accessed | tf_op | source)
XLA Modules:
  0.0 385.2 jit_solution(12614044822953485325)
XLA Ops:
  7.2 2.4 copy.87
  9.6 11.1 %all-to-all-start = ((bf16[128,32,1,128]{0,3,2,1:T(8,128)(2,1)}), bf16[128,32,1,128]{0,3,2,1:T(8,128)(2,1)S(1)}, u32[]{:S(2)}, u32[]{:S(2)}) async-start(bf16[128,32,1,128]{0,3,2,1:T(8,128)(2,1)} %bitcast.143), calls=%async_computation | async-start | bytes 2097152 | tf_op jit(solution)/shard_map/all_to_all | solution.py:80
  20.7 1.3 copy.90
  22.1 25.2 %all-to-all-done = bf16[128,32,1,128]{0,3,2,1:T(8,128)(2,1)S(1)} async-done(((bf16[128,32,1,128]{0,3,2,1:T(8,128)(2,1)}), bf16[128,32,1,128]{0,3,2,1:T(8,128)(2,1)S(1)}, u32[]{:S(2)}, u32[]{:S(2)}) %all-to-all-start) | async-done | bytes 1048608 | tf_op jit(solution)/shard_map/all_to_all | solution.py:80
  48.2 6.4 %all-to-all-start.1 = ((bf16[128,32,1,128]{0,3,2,1:T(8,128)(2,1)}), bf16[128,32,1,128]{0,3,2,1:T(8,128)(2,1)}, u32[]{:S(2)}, u32[]{:S(2)}) async-start(bf16[128,32,1,128]{0,3,2,1:T(8,128)(2,1)} %bitcast.142), calls=%async_computation.1 | async-start | bytes 2097152 | tf_op jit(solution)/shard_map/all_to_all | solution.py:83
  54.7 2.4 copy.93
  57.1 24.1 %all-to-all-done.1 = bf16[128,32,1,128]{0,3,2,1:T(8,128)(2,1)} async-done(((bf16[128,32,1,128]{0,3,2,1:T(8,128)(2,1)}), bf16[128,32,1,128]{0,3,2,1:T(8,128)(2,1)}, u32[]{:S(2)}, u32[]{:S(2)}) %all-to-all-start.1) | async-done | bytes 1048608 | tf_op jit(solution)/shard_map/all_to_all | solution.py:83
  81.2 6.6 %all-to-all-start.2 = ((bf16[128,32,1,128]{0,3,2,1:T(8,128)(2,1)}), bf16[128,32,1,128]{0,3,2,1:T(8,128)(2,1)}, u32[]{:S(2)}, u32[]{:S(2)}) async-start(bf16[128,32,1,128]{0,3,2,1:T(8,128)(2,1)} %bitcast.141), calls=%async_computation.2 | async-start | bytes 2097152 | tf_op jit(solution)/shard_map/all_to_all | solution.py:84
  88.3 1.7 fusion.15
  91.0 1.5 pad_maximum_fusion.1
  92.5 2.3 collective-permute-start.1
  94.9 3.6 collective-permute-start
  100.4 1.6 copy.92
  102.1 12.5 %all-to-all-done.2 = bf16[128,32,1,128]{0,3,2,1:T(8,128)(2,1)} async-done(((bf16[128,32,1,128]{0,3,2,1:T(8,128)(2,1)}), bf16[128,32,1,128]{0,3,2,1:T(8,128)(2,1)}, u32[]{:S(2)}, u32[]{:S(2)}) %all-to-all-start.2) | async-done | bytes 1048608 | tf_op jit(solution)/shard_map/all_to_all | solution.py:84
  114.6 2.3 copy.95
  116.9 55.0 %while.10 = (s32[]{:T(128)}, bf16[8,512,1,128]{3,1,2,0:T(8,128)(2,1)}, bf16[8,512,1,128]{3,1,2,0:T(8,128)(2,1)}, bf16[4096,1,128]{2,0,1:T(8,128)(2,1)S(1)}, bf16[4096,1,128]{2,0,1:T(8,128)(2,1)}, /*index=5*/s32[]{:T(128)}) while((s32[]{:T(128)}, bf16[8,512,1,128]{3,1,2,0:T(8,128)(2,1)}, bf16[8,512,1,128]{3,1,2,0:T(8,128)(2,1)}, ...), condition=%wide.region_6.7_spmd, body=%wide.region_3.0_spmd.sunk | while | flops 1092680704 | bytes 31729776 | solution.py:51
  116.9 2.2 multiply_reduce_fusion.2
  119.1 1.5 fusion.70
  120.6 3.1 fusion.71
  123.7 2.2 multiply_reduce_fusion.2
  126.0 1.5 fusion.70
  127.5 3.1 fusion.71
  130.6 2.2 multiply_reduce_fusion.2
  132.9 1.5 fusion.70
  134.4 3.1 fusion.71
  137.5 2.2 multiply_reduce_fusion.2
  139.7 1.5 fusion.70
  141.3 3.1 fusion.71
  144.4 2.2 multiply_reduce_fusion.2
  146.6 1.5 fusion.70
  148.1 3.1 fusion.71
  151.3 2.2 multiply_reduce_fusion.2
  153.5 1.5 fusion.70
  155.0 3.1 fusion.71
  158.1 2.2 multiply_reduce_fusion.2
  160.4 1.5 fusion.70
  161.9 3.1 fusion.71
  165.0 2.2 multiply_reduce_fusion.2
  167.3 1.5 fusion.70
  168.8 3.1 fusion.71
  172.4 3.4 reduce.4
  175.8 2.1 reshape.88
  178.0 6.3 %all-to-all-start.3 = ((bf16[32,2,8192]{2,1,0:T(2,128)(2,1)}), bf16[32,2,8192]{2,1,0:T(2,128)(2,1)}, u32[]{:S(2)}, u32[]{:S(2)}) async-start(bf16[32,2,8192]{2,1,0:T(2,128)(2,1)} %reshape.88), calls=%async_computation.3 | async-start | bytes 2097152 | tf_op jit(solution)/shard_map/all_to_all | solution.py:87
  184.6 3.5 pad_maximum_fusion
  188.1 2.4 slice_bitcast_fusion
  190.5 2.5 copy.106
  193.0 4.8 %copy.104 = bf16[1,384,4096]{1,2,0:T(8,128)(2,1)} copy(bf16[1,384,4096]{2,1,0:T(8,128)(2,1)} %get-tuple-element.90) | data formatting | bytes 6291456 | tf_op jit(solution)/shard_map/reshape;squeeze | solution.py:103
  197.8 3.6 fusion.16
  201.4 1.9 fusion.35
  203.3 2.7 copy-done.16
  205.9 2.7 bitcast_convert_fusion
  208.6 2.3 all-to-all-done.3
  210.9 4.3 %reshape.89 = bf16[4096,1,1,128]{3,2,1,0:T(2,128)(2,1)S(1)} reshape(bf16[32,2,8192]{2,1,0:T(2,128)(2,1)} %all-to-all-done.3) | data formatting | bytes 2097152
  216.4 1.5 copy.99
  217.8 4.9 %convolution_bitcast_fusion.3 = f32[384,32,128]{0,2,1:T(8,128)S(1)} fusion(f32[32,128,1,1,128]{1,4,0,3,2:T(8,128)S(1)} %copy.99, f32[32,128,128]{2,1,0:T(8,128)} %get-tuple-element.96, f32[32,128,384]{1,2,0:T(8,128)} %copy-done.16, f32[32,128]{1,0:T(8,128)S(1)} %get-tuple-element.93), kind=kOutput, calls=%fused_computation.33 | convolution fusion | flops 407371776 | bytes 16793600 | tf_op jit(solution)/shard_map/hqk,qhd->khd/dot_general | solution.py:133
  223.4 4.2 %collective-permute-start.2 = (f32[128,4096]{0,1:T(8,128)S(1)}, f32[128,4096]{0,1:T(8,128)S(1)}, u32[]{:S(2)}, u32[]{:S(2)}) collective-permute-start(f32[128,4096]{0,1:T(8,128)S(1)} %bitcast.147), channel_id=1, source_target_pairs={{1,0},{2,1},{3,2},{4,3},{5,4},{6,5},{7,6},{8,7},{9,8},{10,9},{11,1... | collective-permute-start | bytes 6291464 | tf_op jit(solution)/shard_map/ppermute | solution.py:25
  227.6 4.0 %collective-permute-start.3 = (f32[128,4096]{0,1:T(8,128)S(1)}, f32[128,4096]{0,1:T(8,128)S(1)}, u32[]{:S(2)}, u32[]{:S(2)}) collective-permute-start(f32[128,4096]{0,1:T(8,128)S(1)} %bitcast.146), channel_id=1, source_target_pairs={{0,1},{1,2},{2,3},{3,4},{4,5},{5,6},{6,7},{7,8},{8,9},{9,10},{10,1... | collective-permute-start | bytes 6291464 | tf_op jit(solution)/shard_map/ppermute | solution.py:25
  233.2 1.3 fusion.37
  234.5 18.7 %collective-permute-done.2 = f32[128,4096]{0,1:T(8,128)S(1)} collective-permute-done((f32[128,4096]{0,1:T(8,128)S(1)}, f32[128,4096]{0,1:T(8,128)S(1)}, u32[]{:S(2)}, u32[]{:S(2)}) %collective-permute-start.2) | collective-permute-done | bytes 2097184 | tf_op jit(solution)/shard_map/ppermute | solution.py:25
  256.3 1.3 fusion.39
  257.6 1.3 fusion.41
  259.0 1.7 fusion.21
  262.0 114.9 %reduce-scatter.2.cloned.1.call-done = f32[128,128]{0,1:T(8,128)} async-done(((f32[4096,128]{0,1:T(8,128)}), f32[128,128]{0,1:T(8,128)}) %reduce-scatter.2.cloned.1.call-update) | async-done | bytes 65552 | tf_op jit(solution)/shard_map/reduce_scatter | solution.py:160
  376.9 1.4 fusion.34
  (70 shorter events, 12.8 us)
Async XLA Ops:
  7.2 80.6 %copy-start = (bf16[128,4096]{1,0:T(8,128)(2,1)S(1)}, bf16[128,4096]{1,0:T(8,128)(2,1)}, u32[]{:S(2)}) copy-start(bf16[128,4096]{1,0:T(8,128)(2,1)} %param.12) | copy-start | bytes 3145732
  7.2 13.6 %copy-start.1 = (bf16[128,4096]{1,0:T(8,128)(2,1)S(1)}, bf16[128,4096]{1,0:T(8,128)(2,1)}, u32[]{:S(2)}) copy-start(bf16[128,4096]{1,0:T(8,128)(2,1)} %param.10) | copy-start | bytes 3145732
  9.6 37.7 %all-to-all-start = ((bf16[128,32,1,128]{0,3,2,1:T(8,128)(2,1)}), bf16[128,32,1,128]{0,3,2,1:T(8,128)(2,1)S(1)}, u32[]{:S(2)}, u32[]{:S(2)}) async-start(bf16[128,32,1,128]{0,3,2,1:T(8,128)(2,1)} %bitcast.143), calls=%async_computation | async-start | bytes 2097152 | tf_op jit(solution)/shard_map/all_to_all | solution.py:80
  47.3 1.0 copy-start.7
  48.2 33.0 %all-to-all-start.1 = ((bf16[128,32,1,128]{0,3,2,1:T(8,128)(2,1)}), bf16[128,32,1,128]{0,3,2,1:T(8,128)(2,1)}, u32[]{:S(2)}, u32[]{:S(2)}) async-start(bf16[128,32,1,128]{0,3,2,1:T(8,128)(2,1)} %bitcast.142), calls=%async_computation.1 | async-start | bytes 2097152 | tf_op jit(solution)/shard_map/all_to_all | solution.py:83
  54.7 33.1 %copy-start.12 = (bf16[4096,64]{0,1:T(8,128)(2,1)S(1)}, bf16[4096,64]{0,1:T(8,128)(2,1)}, u32[]{:S(2)}) copy-start(bf16[4096,64]{0,1:T(8,128)(2,1)} %param.13) | copy-start | bytes 1572868
  54.7 33.6 %copy-start.4 = (bf16[4096,64]{0,1:T(8,128)(2,1)S(1)}, bf16[4096,64]{0,1:T(8,128)(2,1)}, u32[]{:S(2)}) copy-start(bf16[4096,64]{0,1:T(8,128)(2,1)} %param.14) | copy-start | bytes 1572868
  81.2 33.3 %all-to-all-start.2 = ((bf16[128,32,1,128]{0,3,2,1:T(8,128)(2,1)}), bf16[128,32,1,128]{0,3,2,1:T(8,128)(2,1)}, u32[]{:S(2)}, u32[]{:S(2)}) async-start(bf16[128,32,1,128]{0,3,2,1:T(8,128)(2,1)} %bitcast.141), calls=%async_computation.2 | async-start | bytes 2097152 | tf_op jit(solution)/shard_map/all_to_all | solution.py:84
  88.3 1.7 copy-start.13
  88.3 10.2 %copy-start.15 = (s32[2,4]{1,0:T(2,128)S(1)}, s32[2,4]{1,0:T(2,128)}, u32[]{:S(2)}) copy-start(s32[2,4]{1,0:T(2,128)} %param.15) | copy-start | bytes 100
  90.0 1.0 copy-start.2
  90.1 9.1 %copy-start.8 = (bf16[128,32,1,128]{0,3,2,1:T(8,128)(2,1)S(1)}, bf16[128,32,1,128]{0,3,2,1:T(8,128)(2,1)}, u32[]{:S(2)}) copy-start(bf16[128,32,1,128]{0,3,2,1:T(8,128)(2,1)} %copy-done.7) | copy-start | bytes 3145732
  92.5 92.0 %collective-permute-start.1 = (bf16[2,128,4096]{2,1,0:T(8,128)(2,1)}, bf16[2,128,4096]{2,1,0:T(8,128)(2,1)}, u32[]{:S(2)}, u32[]{:S(2)}) collective-permute-start(bf16[2,128,4096]{2,1,0:T(8,128)(2,1)} %pad_maximum_fusion.1), channel_id=1, source_target_pairs={{1,0},{2,1},{3,2},{4,3},{5,4},{6,5},{7,6},{8,7},{9,8},{10,9},{11,1... | collective-permute-start | bytes 6291464 | tf_op jit(solution)/shard_map/ppermute | solution.py:17
  94.9 89.7 %collective-permute-start = (bf16[2,128,4096]{2,1,0:T(8,128)(2,1)}, bf16[2,128,4096]{2,1,0:T(8,128)(2,1)}, u32[]{:S(2)}, u32[]{:S(2)}) collective-permute-start(bf16[2,128,4096]{2,1,0:T(8,128)(2,1)} %pad_maximum_fusion.1), channel_id=1, source_target_pairs={{0,1},{1,2},{2,3},{3,4},{4,5},{5,6},{6,7},{7,8},{8,9},{9,10},{10,1... | collective-permute-start | bytes 6291464 | tf_op jit(solution)/shard_map/ppermute | solution.py:14
  119.1 1.5 copy-start.11
  126.0 1.5 copy-start.11
  132.9 1.5 copy-start.11
  139.7 1.5 copy-start.11
  146.6 1.5 copy-start.11
  153.5 1.5 copy-start.11
  160.4 1.5 copy-start.11
  167.3 1.5 copy-start.11
  172.4 12.2 %copy-start.3 = (bf16[1,128,4096]{2,1,0:T(8,128)(2,1)S(1)}, bf16[1,128,4096]{2,1,0:T(8,128)(2,1)}, u32[]{:S(2)}) copy-start(bf16[1,128,4096]{2,1,0:T(8,128)(2,1)} %copy-done.2) | copy-start | bytes 3145732
  178.0 32.9 %all-to-all-start.3 = ((bf16[32,2,8192]{2,1,0:T(2,128)(2,1)}), bf16[32,2,8192]{2,1,0:T(2,128)(2,1)}, u32[]{:S(2)}, u32[]{:S(2)}) async-start(bf16[32,2,8192]{2,1,0:T(2,128)(2,1)} %reshape.88), calls=%async_computation.3 | async-start | bytes 2097152 | tf_op jit(solution)/shard_map/all_to_all | solution.py:87
  184.3 192.6 %reduce-scatter.2.cloned.1.call-start = ((), (), s32[]{:S(2)}) async-start(), calls=%async_computation.5 | async-start | bytes 2162688 | tf_op jit(solution)/shard_map/reduce_scatter | solution.py:160
  193.0 4.8 %copy-start.6 = (bf16[128,4096]{1,0:T(8,128)(2,1)S(1)}, bf16[128,4096]{1,0:T(8,128)(2,1)}, u32[]{:S(2)}) copy-start(bf16[128,4096]{1,0:T(8,128)(2,1)} %param.9) | copy-start | bytes 3145732
  201.4 4.5 %copy-start.9 = (bf16[1,384,4096]{1,2,0:T(8,128)(2,1)S(1)}, bf16[1,384,4096]{1,2,0:T(8,128)(2,1)}, u32[]{:S(2)}) copy-start(bf16[1,384,4096]{1,2,0:T(8,128)(2,1)} %copy.104) | copy-start | bytes 9437188
  203.3 2.7 copy-start.16
  222.7 9.0 %copy-start.5 = (bf16[4096,64]{0,1:T(8,128)(2,1)S(1)}, bf16[4096,64]{0,1:T(8,128)(2,1)}, u32[]{:S(2)}) copy-start(bf16[4096,64]{0,1:T(8,128)(2,1)} %param.14) | copy-start | bytes 1572868
  223.4 9.8 %copy-start.14 = (bf16[128,64]{0,1:T(8,128)(2,1)S(1)}, bf16[128,64]{0,1:T(8,128)(2,1)}, u32[]{:S(2)}) copy-start(bf16[128,64]{0,1:T(8,128)(2,1)} %copy-done.13) | copy-start | bytes 49156
  223.4 29.8 %collective-permute-start.2 = (f32[128,4096]{0,1:T(8,128)S(1)}, f32[128,4096]{0,1:T(8,128)S(1)}, u32[]{:S(2)}, u32[]{:S(2)}) collective-permute-start(f32[128,4096]{0,1:T(8,128)S(1)} %bitcast.147), channel_id=1, source_target_pairs={{1,0},{2,1},{3,2},{4,3},{5,4},{6,5},{7,6},{8,7},{9,8},{10,9},{11,1... | collective-permute-start | bytes 6291464 | tf_op jit(solution)/shard_map/ppermute | solution.py:25
  227.6 27.1 %collective-permute-start.3 = (f32[128,4096]{0,1:T(8,128)S(1)}, f32[128,4096]{0,1:T(8,128)S(1)}, u32[]{:S(2)}, u32[]{:S(2)}) collective-permute-start(f32[128,4096]{0,1:T(8,128)S(1)} %bitcast.146), channel_id=1, source_target_pairs={{0,1},{1,2},{2,3},{3,4},{4,5},{5,6},{6,7},{7,8},{8,9},{9,10},{10,1... | collective-permute-start | bytes 6291464 | tf_op jit(solution)/shard_map/ppermute | solution.py:25
  259.0 1.7 copy-start.10
Sparse Core Ops, SparseCore 0:
  260.8 116.0 reduce-scatter.1
where the time goes:
time: 389 us; the launch traced here: 385 us
  waiting for transfers between devices  198 us (51%)
  matrix products  64.6 us (17%)
  starting transfers between devices  44.9 us (12%)
  local copies, waits for them, and re-layouts  39.3 us (10%)
  other arithmetic  24.1 us (6%)
  between operations  14.4 us (4%)
    reduce_scatter x1, waiting for transfers between devices, local(): lax.psum_scatter(summed, 'context', scatter_dimension=0, tiled=True)  115 us
    all_to_all x1, waiting for transfers between devices, local(): lax.all_to_all(split_heads(queries), 'context', split_axis=1, concat_axis...  25.2 us
    dot_general x8, matrix products, one_block(): jnp.einsum('hqk,khd->qhd', weights, values, preferred_element_type=jnp.fl...  25 us
    all_to_all x1, waiting for transfers between devices, local(): lax.all_to_all(split_heads(keys), 'context', split_axis=1, concat_axis=0,...  24.1 us
    unnamed x40, local copies, waits for them, and re-layouts  23.5 us
    ppermute x2, waiting for transfers between devices, shifted(): return lax.ppermute(block, axis, route)  18.7 us
    dot_general x8, matrix products, one_block(): jnp.einsum('qhd,khd->hqk', query_block, keys, preferred_element_type=jnp....  17.9 us
    all_to_all x1, waiting for transfers between devices, local(): lax.all_to_all(split_heads(values), 'context', split_axis=1, concat_axis=...  12.5 us
  transfers between devices with their start and end apart: 9, of which 6 were waited for; matrix products, arithmetic and copies ran while one was open for 26% of the time, Pallas kernels for 0%

commit v1 on v0

v1 whole, which is shorter than its diff:
```python
import functools
import math

import jax
import jax.numpy as jnp
from jax import lax
from jax.experimental import pallas as pl
from jax.experimental.pallas import tpu as pltpu
from jax.sharding import PartitionSpec as P

MESH = pl.DeviceIdType.MESH
F32 = jnp.float32
BF16 = jnp.bfloat16

N = 32
NZ = 8
TOK = 128
HD = 128
RANK = 64
TILE = 64
TOKENS = N * TOK
WIDTH = N * HD
PAD = TOK
DROWS = 80
BQ = 2 * TOK
CK = 512
CV = 1024
EXP2_SCALE = math.log2(math.e) / math.sqrt(HD)


def ring_step(j):
    half = (j + 1) // 2
    return lax.rem(half * lax.rem(j, 2) + (NZ - half) * (1 - lax.rem(j, 2)), NZ)


def dot(a, b):
    return jnp.dot(a, b, preferred_element_type=F32)


def dot_tt(a, b, dims):
    return lax.dot_general(a, b, (dims, ((), ())), preferred_element_type=F32)


def kernel(
    q_hbm,
    k_hbm,
    v_hbm,
    x_hbm,
    down_hbm,
    up_hbm,
    nb_ref,
    out_hbm,
    gdown_ref,
    gup_ref,
    xbuf,
    dwbuf,
    upbuf,
    kbuf,
    vbuf,
    qbuf,
    keys_t,
    v_aug,
    svd,
    expand,
    scores,
    obuf,
    dbuf,
    hid,
    gup_t,
    gdn,
    rs_s1,
    rs_r1,
    rs_s2,
    rs_r2,
    load_sem,
    ssem,
    ksem,
    vsem,
    qsem,
    osem,
    dsem_s,
    dsem_a,
    dsem_b,
    rs_sem,
):
    me = lax.axis_index("context")
    y, z, c = me // 16, lax.rem(me // 2, NZ), lax.rem(me, 2)
    chip = me // 2
    lane = y * 2 + c

    def device(yy, zz, cc):
        return (yy * NZ + zz) * 2 + cc

    def remote(src, dst, send, recv, target):
        return pltpu.make_async_remote_copy(
            src_ref=src,
            dst_ref=dst,
            send_sem=send,
            recv_sem=recv,
            device_id={"context": target},
            device_id_type=MESH,
        )

    def cols(index):
        return pl.ds(pl.multiple_of(index * HD, HD), HD)

    def rows(index, count=TOK):
        return pl.ds(pl.multiple_of(index * TOK, TOK), count)

    def drain(ref, sem):
        pltpu.make_async_copy(ref, ref, sem).wait()

    load_x = pltpu.make_async_copy(x_hbm, xbuf, load_sem.at[0])
    load_dw = pltpu.make_async_copy(down_hbm, dwbuf, load_sem.at[1])
    load_up = pltpu.make_async_copy(up_hbm.at[rows(me)], upbuf, load_sem.at[2])
    load_x.start()
    load_dw.start()
    load_up.start()

    barrier = pltpu.get_barrier_semaphore()

    @pl.loop(1, N)
    def _(j):
        pl.semaphore_signal(
            barrier, inc=1, device_id={"context": lax.rem(me + j, N)}, device_id_type=MESH
        )

    for hbm, buf, sems in ((k_hbm, kbuf, ksem), (v_hbm, vbuf, vsem), (q_hbm, qbuf, qsem)):
        pltpu.make_async_copy(hbm.at[:, cols(me)], buf.at[rows(me)], sems.at[me]).start()

    keys_t[:, :PAD] = jnp.zeros((HD, PAD), BF16)
    keys_t[:, PAD + TOKENS :] = jnp.zeros((HD, PAD), BF16)
    svd[:PAD, :] = jnp.zeros((PAD, 2 * HD), BF16)
    svd[PAD + TOKENS :, :] = jnp.zeros((PAD, 2 * HD), BF16)
    hid[...] = jnp.zeros_like(hid)
    gup_t[...] = jnp.zeros_like(gup_t)
    slot_row = lax.broadcasted_iota(jnp.int32, (TOK, 3 * TOK), 0)
    slot_col = lax.broadcasted_iota(jnp.int32, (TOK, 3 * TOK), 1)
    expand[...] = jnp.where(slot_row - RANK == slot_col // TILE, 1.0, 0.0).astype(BF16)

    @pl.loop(0, N)
    def _(s):
        v_aug[rows(s), HD:] = jnp.ones((TOK, HD), BF16)

    load_x.wait()
    load_dw.wait()
    load_up.wait()
    down = dot(xbuf[...], dwbuf[...])
    mask_row = lax.broadcasted_iota(jnp.int32, (DROWS - RANK, TOK), 0)
    mask_col = lax.broadcasted_iota(jnp.int32, (DROWS - RANK, TOK), 1)
    mask = jnp.zeros((DROWS - RANK, TOK), F32)
    for slot in range(6):
        wanted = (me - 1) * 2 + slot
        seen = []
        for t in range(2):
            hit = jnp.float32(0.0)
            for e in range(4):
                hit = jnp.where(nb_ref[t, e] == wanted, jnp.float32(1.0), hit)
            seen.append(hit)
        mask = jnp.where(
            mask_row == slot, jnp.where(mask_col < TILE, seen[0], seen[1]), mask
        )
    dbuf[lane, z, :RANK, :] = down.T.astype(BF16)
    dbuf[lane, z, RANK:, :] = mask.astype(BF16)
    up = upbuf[...]

    pl.semaphore_wait(barrier, N - 1)

    @pl.loop(1, NZ)
    def _(j):
        remote(
            dbuf.at[lane, z],
            dbuf.at[lane, z],
            dsem_s.at[0],
            dsem_a,
            device(y, lax.rem(z + ring_step(j), NZ), c),
        ).start()

    def send_all(hbm, buf, send, sems):
        @pl.loop(1, N)
        def _(i):
            target = device(
                lax.rem(y + lax.rem(i // 2, 2), 2),
                lax.rem(z + ring_step(i // 4), NZ),
                lax.rem(c + lax.rem(i, 2), 2),
            )
            remote(hbm.at[:, cols(target)], buf.at[rows(me)], send, sems.at[me], target).start()

    send_all(k_hbm, kbuf, ssem.at[0], ksem)

    drain(dbuf.at[0, pl.ds(0, NZ - 1)], dsem_a)
    for dy, dc in ((0, 1), (1, 0), (1, 1)):
        remote(
            dbuf.at[lane],
            dbuf.at[lane],
            dsem_s.at[1],
            dsem_b.at[lane],
            device(lax.rem(y + dy, 2), z, lax.rem(c + dc, 2)),
        ).start()

    send_all(v_hbm, vbuf, ssem.at[1], vsem)
    send_all(q_hbm, qbuf, ssem.at[2], qsem)

    def source(i):
        return device(
            lax.rem(y + lax.rem(i // 2, 2), 2),
            lax.rem(z + NZ - ring_step(i // 4), NZ),
            lax.rem(c + lax.rem(i, 2), 2),
        )

    @pl.loop(0, N)
    def _(i):
        s = source(i)
        drain(kbuf.at[rows(s)], ksem.at[s])
        keys_t[:, rows(s + 1)] = kbuf[rows(s), :].T

    for dy, dc in ((0, 1), (1, 0), (1, 1)):
        other = lax.rem(y + dy, 2) * 2 + lax.rem(c + dc, 2)
        drain(dbuf.at[other], dsem_b.at[other])

    @pl.loop(0, N)
    def _(i):
        s = source(i)
        block = dbuf[
            (s // 16) * 2 + lax.rem(s, 2), lax.rem(s // 2, NZ)
        ]
        block = jnp.concatenate([block, jnp.zeros((TOK - DROWS, TOK), BF16)], axis=0).T
        drain(vbuf.at[rows(s)], vsem.at[s])
        value = vbuf[rows(s), :]
        v_aug[rows(s), :HD] = value
        term = dot_tt(block[:, :RANK], up, ((1,), (1,)))
        svd[rows(s + 1), :HD] = (value.astype(F32) + term).astype(BF16)
        svd[rows(s + 1), HD:] = block

    up_t = up.T

    @pl.loop(0, N // 2)
    def _(i):
        pair = lax.rem(y + lax.rem(i, 2), 2) * NZ + lax.rem(z + NZ - ring_step(i // 2), NZ)
        for u in range(2):
            drain(qbuf.at[rows(2 * pair + u)], qsem.at[2 * pair + u])
        query = qbuf[rows(2 * pair, BQ), :]
        top = None
        for n in range(TOKENS // CK):
            chunk = dot(query, keys_t[:, PAD + n * CK : PAD + (n + 1) * CK])
            scores[:, n * CK : (n + 1) * CK] = chunk
            for m in range(CK // HD):
                part = chunk[:, m * HD : (m + 1) * HD]
                top = part if top is None else jnp.maximum(top, part)
        top = jnp.max(top, axis=1, keepdims=True)
        total = None
        for n in range(TOKENS // CV):
            expo = jnp.exp2((scores[:, n * CV : (n + 1) * CV] - top) * EXP2_SCALE)
            part = dot(expo.astype(BF16), v_aug[n * CV : (n + 1) * CV, :])
            total = part if total is None else total + part
        teacher = (total[:, :HD] / total[:, HD:]).astype(BF16).astype(F32)
        for u in range(2):
            s = 2 * pair + u
            window = rows(s, 3 * TOK)
            raw = dot(qbuf[rows(s), :], keys_t[:, window])
            seen = dot(svd[rows(s + 1), HD:], expand[...])
            raw = jnp.where(seen > 0.5, raw, -1e30)
            high = jnp.max(raw, axis=1, keepdims=True)
            expo = jnp.exp2((raw - high) * EXP2_SCALE)
            weights = (expo / jnp.sum(expo, axis=1, keepdims=True)).astype(BF16)
            mixed = dot(weights, svd[window, :])
            student = mixed[:, :HD]
            obuf[rows(s), :] = student.astype(BF16)
            grad = ((student - teacher[u * TOK : (u + 1) * TOK, :]) * (TOKENS**-0.5)).astype(BF16)
            latent = dot_tt(up_t, grad, ((1,), (1,))).astype(BF16)
            hid[:, window] += dot(latent, weights)
            gup_t[...] += dot_tt(mixed[:, HD : HD + RANK].astype(BF16), grad, ((0,), (0,)))
        for u in range(2):
            s = 2 * pair + u

            @pl.when(s == me)
            def _():
                pltpu.make_async_copy(
                    obuf.at[rows(s)], out_hbm.at[:, cols(me)], osem.at[2]
                ).start()

            @pl.when(s != me)
            def _():
                remote(
                    obuf.at[rows(s)], out_hbm.at[:, cols(me)], osem.at[0], osem.at[1], s
                ).start()

    gup_ref[...] = gup_t[...].T

    def reduce_scatter(src, offset, k):
        def block(owner_chip, owner_core):
            return src[:, pl.ds(pl.multiple_of(offset + (2 * owner_chip + owner_core) * TOK, TOK), TOK)]

        @pl.loop(0, N // 2)
        def _(m):
            rs_s1[k, m] = block(m, 1 - c).astype(BF16)

        copy = remote(rs_s1.at[k], rs_r1.at[k], rs_sem.at[k, 0], rs_sem.at[k, 1], 2 * chip + 1 - c)
        copy.start()
        copy.wait()

        @pl.loop(0, N // 2)
        def _(m):
            rs_s2[k, m] = (block(m, c) + rs_r1[k, m].astype(F32)).astype(BF16)

        @pl.loop(1, N // 2)
        def _(i):
            owner = lax.rem(y + lax.rem(i, 2), 2) * NZ + lax.rem(z + ring_step(i // 2), NZ)
            remote(
                rs_s2.at[k, owner], rs_r2.at[k, chip], rs_sem.at[k, 2], rs_sem.at[k, 3], 2 * owner + c
            ).start()

        rs_r2[k, chip] = rs_s2[k, chip]
        drain(rs_r2.at[k, pl.ds(0, N // 2 - 1)], rs_sem.at[k, 3])
        result = rs_r2[k, 0].astype(F32)
        for m in range(1, N // 2):
            result = result + rs_r2[k, m].astype(F32)
        return result

    hidden = reduce_scatter(hid, PAD, 0)
    hidden_hi = hidden.astype(BF16)
    hidden_lo = (hidden - hidden_hi.astype(F32)).astype(BF16)
    gdn[...] = dot(hidden_hi, xbuf[...]) + dot(hidden_lo, xbuf[...])
    gdown_ref[...] = reduce_scatter(gdn, 0, 1).T

    for a in range(3):
        drain(kbuf.at[pl.ds(0, (N - 1) * TOK)], ssem.at[a])
    drain(dbuf.at[0, pl.ds(0, NZ - 1)], dsem_s.at[0])
    drain(dbuf.at[pl.ds(0, 3)], dsem_s.at[1])
    for k in range(2):
        drain(rs_s2.at[k, pl.ds(0, N // 2 - 1)], rs_sem.at[k, 2])
    drain(obuf.at[pl.ds(0, (N - 1) * TOK)], osem.at[0])
    drain(obuf.at[pl.ds(0, (N - 1) * TOK)], osem.at[1])
    drain(obuf.at[pl.ds(0, TOK)], osem.at[2])


def local(
    queries, keys, values, value_layer_input, adapter_down_weight, adapter_up_weight, neighbors
):
    anywhere = pl.BlockSpec(memory_space=pl.ANY)
    vmem = pl.BlockSpec(memory_space=pltpu.VMEM)
    dma = pltpu.SemaphoreType.DMA
    return pl.pallas_call(
        kernel,
        out_shape=(
            jax.ShapeDtypeStruct((TOK, WIDTH), BF16),
            jax.ShapeDtypeStruct((TOK, RANK), F32),
            jax.ShapeDtypeStruct((TOK, RANK), F32),
        ),
        in_specs=[anywhere] * 6 + [pl.BlockSpec(memory_space=pltpu.SMEM)],
        out_specs=(anywhere, vmem, vmem),
        scratch_shapes=[
            pltpu.VMEM((TOK, WIDTH), BF16),
            pltpu.VMEM((WIDTH, RANK), BF16),
            pltpu.VMEM((HD, RANK), BF16),
            pltpu.VMEM((TOKENS, HD), BF16),
            pltpu.VMEM((TOKENS, HD), BF16),
            pltpu.VMEM((TOKENS, HD), BF16),
            pltpu.VMEM((HD, TOKENS + 2 * PAD), BF16),
            pltpu.VMEM((TOKENS, 2 * HD), BF16),
            pltpu.VMEM((TOKENS + 2 * PAD, 2 * HD), BF16),
            pltpu.VMEM((TOK, 3 * TOK), BF16),
            pltpu.VMEM((BQ, TOKENS), F32),
            pltpu.VMEM((TOKENS, HD), BF16),
            pltpu.VMEM((4, NZ, DROWS, TOK), BF16),
            pltpu.VMEM((RANK, TOKENS + 2 * PAD), F32),
            pltpu.VMEM((RANK, HD), F32),
            pltpu.VMEM((RANK, WIDTH), F32),
            pltpu.VMEM((2, N // 2, RANK, TOK), BF16),
            pltpu.VMEM((2, N // 2, RANK, TOK), BF16),
            pltpu.VMEM((2, N // 2, RANK, TOK), BF16),
            pltpu.VMEM((2, N // 2, RANK, TOK), BF16),
            dma((3,)),
            dma((3,)),
            dma((N,)),
            dma((N,)),
            dma((N,)),
            dma((3,)),
            dma((2,)),
            dma,
            dma((4,)),
            dma((2, 4)),
        ],
        compiler_params=pltpu.CompilerParams(
            collective_id=0, has_side_effects=True, vmem_limit_bytes=60 << 20
        ),
    )(queries, keys, values, value_layer_input, adapter_down_weight, adapter_up_weight, neighbors)


def solution(mesh):
    rows_split = P(("video", "context"), None)
    return jax.shard_map(
        local,
        mesh=mesh,
        in_specs=(rows_split,) * 4 + (P(), P(), rows_split),
        out_specs=(rows_split,) * 3,
        check_vma=False,
    )
```

time: 389 us -> 150 us (0.39)
  waiting for transfers between devices: 198 us -> 0 us
  Pallas kernels: 0 us -> 140 us
  matrix products: 64.6 us -> 0 us
  starting transfers between devices: 44.9 us -> 0 us
  local copies, waits for them, and re-layouts: 39.3 us -> 8.29 us
  other arithmetic: 24.1 us -> 0 us
  between operations: 14.4 us -> 0.66 us
    pallas_call x0 -> x1, Pallas kernels: none -> 140 us  [local(): pl.pallas_call(kernel, out_shape=(jax.ShapeDtypeStruct((TOK, WIDTH), BF16...]
    reduce_scatter x1 -> x0, waiting for transfers between devices: 115 us -> none  [local(): lax.psum_scatter(summed, 'context', scatter_dimension=0, tiled=True)]
    dot_general x30 -> x0, matrix products: 64.6 us -> none  [the longest x8 25 us: one_block(): jnp.einsum('hqk,khd->qhd', weights, values, preferred_element_type=jnp.fl...]
    all_to_all x4 -> x0, waiting for transfers between devices: 64.1 us -> none  [the longest x1 25.2 us: local(): lax.all_to_all(split_heads(queries), 'context', split_axis=1, concat_axis...]
    all_to_all x4 -> x0, starting transfers between devices: 30.5 us -> none  [the longest x1 11.1 us: local(): lax.all_to_all(split_heads(queries), 'context', split_axis=1, concat_axis...]
    ppermute x4 -> x0, waiting for transfers between devices: 18.7 us -> none  [the longest x2 18.7 us: shifted(): return lax.ppermute(block, axis, route)]
    unnamed x40 -> x7, local copies, waits for them, and re-layouts: 23.5 us -> 6.03 us
    ppermute x4 -> x0, starting transfers between devices: 14.2 us -> none  [the longest x2 8.27 us: shifted(): return lax.ppermute(block, axis, route)]
  transfers between devices with their start and end apart: 9 -> 0, of which waited for: 6 -> 0; matrix products, arithmetic and copies ran while one was open for 26% -> 0% of each run, Pallas kernels for 0% -> 0%
where the time goes in v1:
time: 150 us; the launch traced here: 149 us
  Pallas kernels  140 us (93%)
  local copies, waits for them, and re-layouts  8.29 us (6%)
    pallas_call x1, Pallas kernels, local(): pl.pallas_call(kernel, out_shape=(jax.ShapeDtypeStruct((TOK, WIDTH), BF16...  140 us
    unnamed x7, local copies, waits for them, and re-layouts  6.03 us

profile of v1, /device:TPU:1, one launch (start us, length us, event | category | flops | bytes accessed | tf_op | source)
XLA Modules:
  0.0 148.8 jit_solution(5776199216010200811)
XLA Ops:
  0.6 0.0 copy-start
  0.6 2.4 %copy.10.down_hbm = bf16[4096,64]{1,0:T(8,128)(2,1)} copy(bf16[4096,64]{0,1:T(8,128)(2,1)} %param.11) | data formatting | bytes 1048576 | tf_op args[4]
  3.1 0.0 copy-done
  3.1 1.3 copy.11.up_hbm
  4.4 139.9 %shard_map.94 = (bf16[128,4096]{1,0:T(8,128)(2,1)}, f32[128,64]{1,0:T(8,128)}, f32[128,64]{1,0:T(8,128)}) custom-call(bf16[128,4096]{1,0:T(8,128)(2,1)} %q_hbm.1, bf16[128,4096]{1,0:T(8,128)(2,1)} %k_hbm.1, bf16[128,4096]{1,0:T(8,128)(2,1)} %v_hbm.1, bf16[128,4096]{1,0:T(8,128)(2,1)} %x_hbm.1, bf16[4096,64]{1,0:T(8,128)(2,1)} %copy.10.down_hbm, ...), custom_call_target="tpu_custom_call" | custom-call | tf_op jit(solution)/shard_map/pallas_call | solution.py:343
  144.2 0.0 copy-start.1
  144.2 1.6 %copy.12 = f32[128,64]{0,1:T(8,128)} copy(f32[128,64]{1,0:T(8,128)} %get-tuple-element.4) | data formatting | bytes 65536 | tf_op jit(solution)/shard_map/pallas_call | solution.py:343
  145.8 0.0 copy-done.1
  145.8 0.7 copy.13
  146.5 2.3 %copy.15 = bf16[128,4096]{1,0:T(8,128)(2,1)} copy(bf16[128,4096]{1,0:T(8,128)(2,1)} %get-tuple-element.9) | data formatting | bytes 2097152
Async XLA Ops:
  0.6 2.4 %copy-start = (bf16[4096,64]{0,1:T(8,128)(2,1)S(1)}, bf16[4096,64]{0,1:T(8,128)(2,1)}, u32[]{:S(2)}) copy-start(bf16[4096,64]{0,1:T(8,128)(2,1)} %param.12) | copy-start | bytes 1572868
  144.2 1.6 %copy-start.1 = (f32[128,64]{1,0:T(8,128)S(1)}, f32[128,64]{1,0:T(8,128)}, u32[]{:S(2)}) copy-start(f32[128,64]{1,0:T(8,128)} %get-tuple-element.5) | copy-start | bytes 98308

commit v2 on v1

v2 whole, which is shorter than its diff:
```python
import math

import jax
import jax.numpy as jnp
from jax import lax
from jax.experimental import pallas as pl
from jax.experimental.pallas import tpu as pltpu
from jax.sharding import PartitionSpec as P

MESH = pl.DeviceIdType.MESH
F32 = jnp.float32
BF16 = jnp.bfloat16

N = 32
NZ = 8
TOK = 128
HD = 128
RANK = 64
TILE = 64
TOKENS = N * TOK
WIDTH = N * HD
PAD = TOK
DROWS = 80
BQ = 4 * TOK
CK = 4 * TOK
EXP2_SCALE = math.log2(math.e) / math.sqrt(HD)


def ring_step(j):
    half = (j + 1) // 2
    return lax.rem(half * lax.rem(j, 2) + (NZ - half) * (1 - lax.rem(j, 2)), NZ)


def dot(a, b):
    return jnp.dot(a, b, preferred_element_type=F32)


def dot_tt(a, b, dims):
    return lax.dot_general(a, b, (dims, ((), ())), preferred_element_type=F32)


def kernel(
    q_hbm,
    k_hbm,
    v_hbm,
    x_hbm,
    down_hbm,
    up_hbm,
    nb_ref,
    out_hbm,
    gdown_ref,
    gup_ref,
    xbuf,
    dwbuf,
    up_t,
    kbuf,
    vbuf,
    qbuf,
    keys_t,
    v_aug,
    svd,
    expand,
    scores0,
    scores1,
    tops0,
    tops1,
    high,
    acc,
    wts,
    stu,
    mixd,
    obuf,
    dbuf,
    hid,
    gdn,
    hid_hi,
    hid_lo,
    rs_s1,
    rs_r1,
    rs_s2,
    rs_r2,
    load_sem,
    ssem,
    ksem,
    vsem,
    qsem,
    osem,
    dsem_s,
    dsem_a,
    dsem_b,
    rs_sem,
    rs_pair,
):
    me = lax.axis_index("context")
    y, z, c = me // 16, lax.rem(me // 2, NZ), lax.rem(me, 2)
    chip = me // 2
    lane = y * 2 + c

    def device(yy, zz, cc):
        return (yy * NZ + zz) * 2 + cc

    def remote(src, dst, send, recv, target):
        return pltpu.make_async_remote_copy(
            src_ref=src,
            dst_ref=dst,
            send_sem=send,
            recv_sem=recv,
            device_id={"context": target},
            device_id_type=MESH,
        )

    def cols(index):
        return pl.ds(pl.multiple_of(index * HD, HD), HD)

    def rows(index, count=TOK):
        return pl.ds(pl.multiple_of(index * TOK, TOK), count)

    def drain(ref, sem):
        pltpu.make_async_copy(ref, ref, sem).wait()

    load_x = pltpu.make_async_copy(x_hbm, xbuf, load_sem.at[0])
    load_dw = pltpu.make_async_copy(down_hbm, dwbuf, load_sem.at[1])
    load_up = pltpu.make_async_copy(up_hbm.at[:, cols(me)], up_t, load_sem.at[2])
    load_x.start()
    load_dw.start()
    load_up.start()

    barrier = pltpu.get_barrier_semaphore()

    @pl.loop(1, N)
    def _(j):
        pl.semaphore_signal(
            barrier, inc=1, device_id={"context": lax.rem(me + j, N)}, device_id_type=MESH
        )

    for hbm, buf, sems in ((k_hbm, kbuf, ksem), (v_hbm, vbuf, vsem), (q_hbm, qbuf, qsem)):
        pltpu.make_async_copy(hbm.at[:, cols(me)], buf.at[rows(me)], sems.at[me]).start()

    keys_t[:, :PAD] = jnp.zeros((HD, PAD), BF16)
    keys_t[:, PAD + TOKENS :] = jnp.zeros((HD, PAD), BF16)
    svd[:PAD, :] = jnp.zeros((PAD, 2 * HD), BF16)
    svd[PAD + TOKENS :, :] = jnp.zeros((PAD, 2 * HD), BF16)
    hid[...] = jnp.zeros_like(hid)
    gup_ref[...] = jnp.zeros_like(gup_ref)
    slot_row = lax.broadcasted_iota(jnp.int32, (TOK, 3 * TOK), 0)
    slot_col = lax.broadcasted_iota(jnp.int32, (TOK, 3 * TOK), 1)
    expand[...] = jnp.where(slot_row - RANK == slot_col // TILE, 1.0, 0.0).astype(BF16)

    @pl.loop(0, N)
    def _(s):
        v_aug[rows(s), HD:] = jnp.ones((TOK, HD), BF16)
        high[rows(s), :] = jnp.full((TOK, HD), -1e30, F32)
        acc[rows(s), :] = jnp.zeros((TOK, 2 * HD), F32)

    load_x.wait()
    load_dw.wait()
    load_up.wait()
    mask_row = lax.broadcasted_iota(jnp.int32, (DROWS - RANK, TOK), 0)
    mask_col = lax.broadcasted_iota(jnp.int32, (DROWS - RANK, TOK), 1)
    mask = jnp.zeros((DROWS - RANK, TOK), F32)
    for slot in range(6):
        wanted = (me - 1) * 2 + slot
        seen = []
        for t in range(2):
            hit = jnp.float32(0.0)
            for e in range(4):
                hit = jnp.where(nb_ref[t, e] == wanted, jnp.float32(1.0), hit)
            seen.append(hit)
        mask = jnp.where(
            mask_row == slot, jnp.where(mask_col < TILE, seen[0], seen[1]), mask
        )
    dbuf[lane, z, :RANK, :] = dot_tt(dwbuf[...], xbuf[...], ((1,), (1,))).astype(BF16)
    dbuf[lane, z, RANK:, :] = mask.astype(BF16)

    pl.semaphore_wait(barrier, N - 1)

    @pl.loop(1, NZ)
    def _(j):
        remote(
            dbuf.at[lane, z],
            dbuf.at[lane, z],
            dsem_s.at[0],
            dsem_a,
            device(y, lax.rem(z + ring_step(j), NZ), c),
        ).start()

    def send_all(*arrays):
        @pl.loop(1, N)
        def _(i):
            target = device(
                lax.rem(y + lax.rem(i // 2, 2), 2),
                lax.rem(z + ring_step(i // 4), NZ),
                lax.rem(c + lax.rem(i, 2), 2),
            )
            for hbm, buf, send, sems in arrays:
                remote(
                    hbm.at[:, cols(target)], buf.at[rows(me)], send, sems.at[me], target
                ).start()

    send_all((q_hbm, qbuf, ssem.at[0], qsem))

    drain(dbuf.at[0, pl.ds(0, NZ - 1)], dsem_a)
    for dy, dc in ((0, 1), (1, 0), (1, 1)):
        remote(
            dbuf.at[lane],
            dbuf.at[lane],
            dsem_s.at[1],
            dsem_b.at[lane],
            device(lax.rem(y + dy, 2), z, lax.rem(c + dc, 2)),
        ).start()

    send_all((k_hbm, kbuf, ssem.at[1], ksem), (v_hbm, vbuf, ssem.at[2], vsem))

    for dy, dc in ((0, 1), (1, 0), (1, 1)):
        other = lax.rem(y + dy, 2) * 2 + lax.rem(c + dc, 2)
        drain(dbuf.at[other], dsem_b.at[other])

    @pl.loop(0, N)
    def _(s):
        drain(qbuf.at[rows(s)], qsem.at[s])

    def position(j):
        return lax.rem(z + NZ - ring_step(j), NZ)

    def send_out(j):
        s = device(lax.rem(j // 2, 2), position(j // 4), lax.rem(j, 2))

        @pl.when(s == me)
        def _():
            pltpu.make_async_copy(obuf.at[rows(s)], out_hbm.at[:, cols(me)], osem.at[2]).start()

        @pl.when(s != me)
        def _():
            remote(
                obuf.at[rows(s)], out_hbm.at[:, cols(me)], osem.at[0], osem.at[1], s
            ).start()

    def done(k):
        f = (k + 1) // 2
        return (2 * f - 3) * ((f + 2) // 4) + 3 * (k // NZ)

    @pl.loop(0, NZ)
    def _(g):
        place = position(g)
        for yy in range(2):
            for cc in range(2):
                s = device(yy, place, cc)
                drain(kbuf.at[rows(s)], ksem.at[s])
                keys_t[:, rows(s + 1)] = kbuf[rows(s), :].T
                block = jnp.concatenate(
                    [dbuf[yy * 2 + cc, place], jnp.zeros((TOK - DROWS, TOK), BF16)], axis=0
                ).T
                term = dot(block[:, :RANK], up_t[...])
                drain(vbuf.at[rows(s)], vsem.at[s])
                value = vbuf[rows(s), :]
                v_aug[rows(s), :HD] = value
                svd[rows(s + 1), :HD] = (value.astype(F32) + term).astype(BF16)
                svd[rows(s + 1), HD:] = block

        @pl.loop(done(g), done(g + 1))
        def _(j):
            for lane_at in range(4):
                s = device(lane_at // 2, position(j), lane_at % 2)
                window = rows(s, 3 * TOK)
                raw = dot(qbuf[rows(s), :], keys_t[:, window])
                seen = dot(svd[rows(s + 1), HD:], expand[...])
                raw = jnp.where(seen > 0.5, raw, -1e30)
                most = jnp.max(raw, axis=1, keepdims=True)
                expo = jnp.exp2((raw - most) * EXP2_SCALE)
                weights = (expo / jnp.sum(expo, axis=1, keepdims=True)).astype(BF16)
                mixed = dot(weights, svd[window, :])
                wts[s] = weights
                stu[rows(s), :] = mixed[:, :HD]
                obuf[rows(s), :] = mixed[:, :HD].astype(BF16)
                mixd[rows(s), :] = mixed[:, HD:].astype(BF16)

        @pl.loop(4 * done(g), 4 * done(g + 1))
        def _(j):
            send_out(j)

        firsts = [(yy * NZ + place) * 2 for yy in range(2)]

        def score(i, scores, tops):
            block = pl.ds(pl.multiple_of(i * BQ, BQ), BQ)
            query = qbuf[block, :]
            top = high[block, :]
            for yy, first in enumerate(firsts):
                chunk = dot(query, keys_t[:, rows(first + 1, 2 * TOK)])
                scores[:, yy * 2 * TOK : (yy + 1) * 2 * TOK] = chunk
                top = jnp.maximum(top, jnp.maximum(chunk[:, :HD], chunk[:, HD:]))
            tops[...] = jnp.broadcast_to(jnp.max(top, axis=1, keepdims=True), (BQ, HD))

        def update(i, scores, tops):
            block = pl.ds(pl.multiple_of(i * BQ, BQ), BQ)
            new = tops[...]
            alpha = jnp.exp2((high[block, :] - new) * EXP2_SCALE)
            high[block, :] = new
            part = None
            for yy, first in enumerate(firsts):
                expo = jnp.concatenate(
                    [
                        jnp.exp2(
                            (scores[:, (2 * yy + h) * HD : (2 * yy + h + 1) * HD] - new)
                            * EXP2_SCALE
                        ).astype(BF16)
                        for h in range(2)
                    ],
                    axis=1,
                )
                term = dot(expo, v_aug[rows(first, 2 * TOK), :])
                part = term if part is None else part + term
            acc[block, :HD] = acc[block, :HD] * alpha + part[:, :HD]
            acc[block, HD:] = acc[block, HD:] * alpha + part[:, HD:]

        blocks = TOKENS // BQ
        score(0, scores0, tops0)

        @pl.loop(0, blocks // 2)
        def _(i):
            update(2 * i, scores0, tops0)
            score(2 * i + 1, scores1, tops1)
            update(2 * i + 1, scores1, tops1)
            score(lax.rem(2 * i + 2, blocks), scores0, tops0)

    def block(src, offset, owner):
        return src[:, pl.ds(pl.multiple_of(offset + owner * TOK, TOK), TOK)]

    def exchange(k, src, offset, ch):
        for m in range(4):
            owner = 4 * ch + m
            rs_s1[k, owner] = block(src, offset, 2 * owner + 1 - c).astype(BF16)
        part = pl.ds(4 * ch, 4)
        remote(
            rs_s1.at[k, part], rs_r1.at[k, part], rs_sem.at[k, 0], rs_pair.at[k, ch], me + 1 - 2 * c
        ).start()

    def scatter(k, src, offset):
        @pl.loop(0, 4)
        def _(ch):
            drain(rs_r1.at[k, pl.ds(4 * ch, 4)], rs_pair.at[k, ch])
            for m in range(4):
                owner = 4 * ch + m
                rs_s2[k, owner] = (
                    block(src, offset, 2 * owner + c) + rs_r1[k, owner].astype(F32)
                ).astype(BF16)

        @pl.loop(1, N // 2)
        def _(i):
            owner = lax.rem(y + lax.rem(i, 2), 2) * NZ + lax.rem(z + ring_step(i // 2), NZ)
            remote(
                rs_s2.at[k, owner], rs_r2.at[k, chip], rs_sem.at[k, 1], rs_sem.at[k, 2], 2 * owner + c
            ).start()

        rs_r2[k, chip] = rs_s2[k, chip]

    def total(k):
        drain(rs_r2.at[k, pl.ds(0, N // 2 - 1)], rs_sem.at[k, 2])
        result = rs_r2[k, 0].astype(F32)
        for m in range(1, N // 2):
            result = result + rs_r2[k, m].astype(F32)
        return result

    @pl.loop(0, 4)
    def _(ch):
        def adapter(s):
            teacher = (acc[rows(s), :HD] / acc[rows(s), HD:]).astype(BF16).astype(F32)
            grad = ((stu[rows(s), :] - teacher) * (TOKENS**-0.5)).astype(BF16)
            latent = dot_tt(up_t[...], grad, ((1,), (1,))).astype(BF16)
            return (
                dot(latent, wts[s]),
                dot_tt(mixd[rows(s), :RANK], grad, ((0,), (0,))),
            )

        @pl.loop(0, 2)
        def _(h):
            slabs = [8 * ch + 4 * h + u for u in range(4)]
            terms = [adapter(s) for s in slabs]
            for s, term in zip(slabs, terms):
                hid[:, rows(s, 3 * TOK)] += term[0]
            gup_ref[...] += (terms[0][1] + terms[1][1]) + (terms[2][1] + terms[3][1])

        @pl.when(ch > 0)
        def _():
            exchange(0, hid, PAD, ch - 1)

    exchange(0, hid, PAD, 3)


    scatter(0, hid, PAD)

    hidden = total(0)
    hid_hi[...] = hidden.astype(BF16)
    hid_lo[...] = (hidden - hidden.astype(BF16).astype(F32)).astype(BF16)

    @pl.loop(0, 4)
    def _(ch):
        part = pl.ds(pl.multiple_of(ch * 8 * TOK, TOK), 8 * TOK)
        gdn[:, part] = dot(hid_hi[...], xbuf[:, part]) + dot(hid_lo[...], xbuf[:, part])
        exchange(1, gdn, 0, ch)

    scatter(1, gdn, 0)
    gdown_ref[...] = total(1)

    for a in range(3):
        drain(kbuf.at[pl.ds(0, (N - 1) * TOK)], ssem.at[a])
    drain(dbuf.at[0, pl.ds(0, NZ - 1)], dsem_s.at[0])
    drain(dbuf.at[pl.ds(0, 3)], dsem_s.at[1])
    for k in range(2):
        drain(rs_s1.at[k], rs_sem.at[k, 0])
        drain(rs_s2.at[k, pl.ds(0, N // 2 - 1)], rs_sem.at[k, 1])
    drain(obuf.at[pl.ds(0, (N - 1) * TOK)], osem.at[0])
    drain(obuf.at[pl.ds(0, (N - 1) * TOK)], osem.at[1])
    drain(obuf.at[pl.ds(0, TOK)], osem.at[2])


def local(
    queries, keys, values, value_layer_input, adapter_down_weight, adapter_up_weight, neighbors
):
    anywhere = pl.BlockSpec(memory_space=pl.ANY)
    vmem = pl.BlockSpec(memory_space=pltpu.VMEM)
    dma = pltpu.SemaphoreType.DMA
    student_out, grad_down, grad_up = pl.pallas_call(
        kernel,
        out_shape=(
            jax.ShapeDtypeStruct((TOK, WIDTH), BF16),
            jax.ShapeDtypeStruct((RANK, HD), F32),
            jax.ShapeDtypeStruct((RANK, HD), F32),
        ),
        in_specs=[anywhere] * 6 + [pl.BlockSpec(memory_space=pltpu.SMEM)],
        out_specs=(anywhere, vmem, vmem),
        scratch_shapes=[
            pltpu.VMEM((TOK, WIDTH), BF16),
            pltpu.VMEM((RANK, WIDTH), BF16),
            pltpu.VMEM((RANK, HD), BF16),
            pltpu.VMEM((TOKENS, HD), BF16),
            pltpu.VMEM((TOKENS, HD), BF16),
            pltpu.VMEM((TOKENS, HD), BF16),
            pltpu.VMEM((HD, TOKENS + 2 * PAD), BF16),
            pltpu.VMEM((TOKENS, 2 * HD), BF16),
            pltpu.VMEM((TOKENS + 2 * PAD, 2 * HD), BF16),
            pltpu.VMEM((TOK, 3 * TOK), BF16),
            pltpu.VMEM((BQ, CK), F32),
            pltpu.VMEM((BQ, CK), F32),
            pltpu.VMEM((BQ, HD), F32),
            pltpu.VMEM((BQ, HD), F32),
            pltpu.VMEM((TOKENS, HD), F32),
            pltpu.VMEM((TOKENS, 2 * HD), F32),
            pltpu.VMEM((N, TOK, 3 * TOK), BF16),
            pltpu.VMEM((TOKENS, HD), F32),
            pltpu.VMEM((TOKENS, HD), BF16),
            pltpu.VMEM((TOKENS, HD), BF16),
            pltpu.VMEM((4, NZ, DROWS, TOK), BF16),
            pltpu.VMEM((RANK, TOKENS + 2 * PAD), F32),
            pltpu.VMEM((RANK, WIDTH), F32),
            pltpu.VMEM((RANK, TOK), BF16),
            pltpu.VMEM((RANK, TOK), BF16),
            pltpu.VMEM((2, N // 2, RANK, TOK), BF16),
            pltpu.VMEM((2, N // 2, RANK, TOK), BF16),
            pltpu.VMEM((2, N // 2, RANK, TOK), BF16),
            pltpu.VMEM((2, N // 2, RANK, TOK), BF16),
            dma((3,)),
            dma((3,)),
            dma((N,)),
            dma((N,)),
            dma((N,)),
            dma((3,)),
            dma((2,)),
            dma,
            dma((4,)),
            dma((2, 3)),
            dma((2, 4)),
        ],
        compiler_params=pltpu.CompilerParams(
            collective_id=0, has_side_effects=True, vmem_limit_bytes=60 << 20
        ),
    )(
        queries,
        keys,
        values,
        value_layer_input,
        adapter_down_weight.T,
        adapter_up_weight.T,
        neighbors,
    )
    return student_out, grad_down.T, grad_up.T


def solution(mesh):
    rows_split = P(("video", "context"), None)
    return jax.shard_map(
        local,
        mesh=mesh,
        in_specs=(rows_split,) * 4 + (P(), P(), rows_split),
        out_specs=(rows_split,) * 3,
        check_vma=False,
    )
```

time: 150 us -> 137 us (0.913)
  Pallas kernels: 140 us -> 132 us
  local copies, waits for them, and re-layouts: 8.29 us -> 3.68 us
    pallas_call x1, Pallas kernels: 140 us -> 132 us  [local(): pl.pallas_call(kernel, out_shape=(jax.ShapeDtypeStruct((TOK, WIDTH), BF16...]
    unnamed x7, local copies, waits for them, and re-layouts: 6.03 us -> 3.68 us
    pallas_call x2 -> x0, local copies, waits for them, and re-layouts: 2.27 us -> none  [local(): pl.pallas_call(kernel, out_shape=(jax.ShapeDtypeStruct((TOK, WIDTH), BF16...]
where the time goes in v2:
time: 137 us
  Pallas kernels  132 us (96%)
  local copies, waits for them, and re-layouts  3.68 us (3%)
    pallas_call x1, Pallas kernels, local(): pl.pallas_call(kernel, out_shape=(jax.ShapeDtypeStruct((TOK, WIDTH), BF16...  132 us
    unnamed x7, local copies, waits for them, and re-layouts  3.68 us

profile of v2, /device:TPU:1, one launch (start us, length us, event | category | flops | bytes accessed | tf_op | source)
XLA Modules:
  0.0 136.6 jit_solution(10618312758255121826)
XLA Ops:
  0.6 132.3 %shard_map.94 = (bf16[128,4096]{1,0:T(8,128)(2,1)}, f32[64,128]{1,0:T(8,128)}, f32[64,128]{1,0:T(8,128)}) custom-call(bf16[128,4096]{1,0:T(8,128)(2,1)} %q_hbm.1, bf16[128,4096]{1,0:T(8,128)(2,1)} %k_hbm.1, bf16[128,4096]{1,0:T(8,128)(2,1)} %v_hbm.1, bf16[128,4096]{1,0:T(8,128)(2,1)} %x_hbm.1, bf16[64,4096]{1,0:T(8,128)(2,1)} %bitcast.4, ...), custom_call_target="tpu_custom_call" | custom-call | tf_op jit(solution)/shard_map/pallas_call | solution.py:422
  132.9 0.0 copy-start.1
  132.9 2.3 %copy.13 = bf16[128,4096]{1,0:T(8,128)(2,1)} copy(bf16[128,4096]{1,0:T(8,128)(2,1)} %get-tuple-element.12) | data formatting | bytes 2097152
  135.2 0.0 copy-done.1
  135.2 0.0 copy-start
  135.2 0.6 copy.14
  135.8 0.2 copy-done
  136.0 0.6 copy.15
Async XLA Ops:
  132.9 2.3 %copy-start.1 = (f32[64,128]{1,0:T(8,128)S(1)}, f32[64,128]{1,0:T(8,128)}, u32[]{:S(2)}) copy-start(f32[64,128]{1,0:T(8,128)} %get-tuple-element.7) | copy-start | bytes 98308
  135.2 0.8 copy-start

commit v3 on v2

--- a/solution.py
+++ b/solution.py
@@ -259,20 +259,21 @@
 
         @pl.loop(done(g), done(g + 1))
         def _(j):
-            for lane_at in range(4):
-                s = device(lane_at // 2, position(j), lane_at % 2)
-                window = rows(s, 3 * TOK)
-                raw = dot(qbuf[rows(s), :], keys_t[:, window])
-                seen = dot(svd[rows(s + 1), HD:], expand[...])
-                raw = jnp.where(seen > 0.5, raw, -1e30)
-                most = jnp.max(raw, axis=1, keepdims=True)
-                expo = jnp.exp2((raw - most) * EXP2_SCALE)
-                weights = (expo / jnp.sum(expo, axis=1, keepdims=True)).astype(BF16)
-                mixed = dot(weights, svd[window, :])
-                wts[s] = weights
-                stu[rows(s), :] = mixed[:, :HD]
-                obuf[rows(s), :] = mixed[:, :HD].astype(BF16)
-                mixd[rows(s), :] = mixed[:, HD:].astype(BF16)
+            if True:
+                slabs = [device(at // 2, position(j), at % 2) for at in range(4)]
+                seen = [dot(svd[rows(s + 1), HD:], expand[...]) for s in slabs]
+                raw = [dot(qbuf[rows(s), :], keys_t[:, rows(s, 3 * TOK)]) for s in slabs]
+                raw = [jnp.where(m > 0.5, r, -1e30) for m, r in zip(seen, raw)]
+                most = [jnp.max(r, axis=1, keepdims=True) for r in raw]
+                expo = [jnp.exp2((r - m) * EXP2_SCALE) for r, m in zip(raw, most)]
+                norm = [1.0 / jnp.sum(e, axis=1, keepdims=True) for e in expo]
+                weights = [(e * n).astype(BF16) for e, n in zip(expo, norm)]
+                mixed = [dot(w, svd[rows(s, 3 * TOK), :]) for w, s in zip(weights, slabs)]
+                for s, w, m in zip(slabs, weights, mixed):
+                    wts[s] = w
+                    stu[rows(s), :] = m[:, :HD]
+                    obuf[rows(s), :] = m[:, :HD].astype(BF16)
+                    mixd[rows(s), :] = m[:, HD:].astype(BF16)
 
         @pl.loop(4 * done(g), 4 * done(g + 1))
         def _(j):
@@ -315,12 +316,16 @@
         blocks = TOKENS // BQ
         score(0, scores0, tops0)
 
-        @pl.loop(0, blocks // 2)
+        @pl.loop(0, blocks // 2 - 1)
         def _(i):
             update(2 * i, scores0, tops0)
             score(2 * i + 1, scores1, tops1)
             update(2 * i + 1, scores1, tops1)
-            score(lax.rem(2 * i + 2, blocks), scores0, tops0)
+            score(2 * i + 2, scores0, tops0)
+
+        update(blocks - 2, scores0, tops0)
+        score(blocks - 1, scores1, tops1)
+        update(blocks - 1, scores1, tops1)
 
     def block(src, offset, owner):
         return src[:, pl.ds(pl.multiple_of(offset + owner * TOK, TOK), TOK)]
@@ -333,6 +338,10 @@
         remote(
             rs_s1.at[k, part], rs_r1.at[k, part], rs_sem.at[k, 0], rs_pair.at[k, ch], me + 1 - 2 * c
         ).start()
+
+    def chip_at(i):
+        r = N // 2 - 1 - i
+        return lax.rem(y + lax.rem(r, 2), 2) * NZ + lax.rem(z + ring_step(r // 2), NZ)
 
     def scatter(k, src, offset):
         @pl.loop(0, 4)
@@ -344,9 +353,9 @@
                     block(src, offset, 2 * owner + c) + rs_r1[k, owner].astype(F32)
                 ).astype(BF16)
 
-        @pl.loop(1, N // 2)
+        @pl.loop(0, N // 2 - 1)
         def _(i):
-            owner = lax.rem(y + lax.rem(i, 2), 2) * NZ + lax.rem(z + ring_step(i // 2), NZ)
+            owner = chip_at(i)
             remote(
                 rs_s2.at[k, owner], rs_r2.at[k, chip], rs_sem.at[k, 1], rs_sem.at[k, 2], 2 * owner + c
             ).start()
@@ -362,22 +371,17 @@
 
     @pl.loop(0, 4)
     def _(ch):
-        def adapter(s):
-            teacher = (acc[rows(s), :HD] / acc[rows(s), HD:]).astype(BF16).astype(F32)
-            grad = ((stu[rows(s), :] - teacher) * (TOKENS**-0.5)).astype(BF16)
-            latent = dot_tt(up_t[...], grad, ((1,), (1,))).astype(BF16)
-            return (
-                dot(latent, wts[s]),
-                dot_tt(mixd[rows(s), :RANK], grad, ((0,), (0,))),
-            )
-
         @pl.loop(0, 2)
         def _(h):
             slabs = [8 * ch + 4 * h + u for u in range(4)]
-            terms = [adapter(s) for s in slabs]
+            span = rows(slabs[0], 4 * TOK)
+            teacher = (acc[span, :HD] / acc[span, HD:]).astype(BF16).astype(F32)
+            grad = ((stu[span, :] - teacher) * (TOKENS**-0.5)).astype(BF16)
+            latent = dot_tt(up_t[...], grad, ((1,), (1,))).astype(BF16)
+            terms = [dot(latent[:, u * TOK : (u + 1) * TOK], wts[s]) for u, s in enumerate(slabs)]
             for s, term in zip(slabs, terms):
-                hid[:, rows(s, 3 * TOK)] += term[0]
-            gup_ref[...] += (terms[0][1] + terms[1][1]) + (terms[2][1] + terms[3][1])
+                hid[:, rows(s, 3 * TOK)] += term
+            gup_ref[...] += dot_tt(mixd[span, :RANK], grad, ((0,), (0,)))
 
         @pl.when(ch > 0)
         def _():
@@ -392,13 +396,38 @@
     hid_hi[...] = hidden.astype(BF16)
     hid_lo[...] = (hidden - hidden.astype(BF16).astype(F32)).astype(BF16)
 
+    def forward(n):
+        drain(rs_r1.at[1, pl.ds(4 * n, 4)], rs_pair.at[1, n])
+        for u in range(4):
+            i = 4 * n + u
+            rs_s2[1, i] = (block(gdn, 0, 2 * i + c) + rs_r1[1, i].astype(F32)).astype(BF16)
+        for u in range(4):
+            i = 4 * n + u
+
+            @pl.when(i < N // 2 - 1)
+            def _():
+                remote(
+                    rs_s2.at[1, i],
+                    rs_r2.at[1, i],
+                    rs_sem.at[1, 1],
+                    rs_sem.at[1, 2],
+                    2 * chip_at(i) + c,
+                ).start()
+
     @pl.loop(0, 4)
-    def _(ch):
-        part = pl.ds(pl.multiple_of(ch * 8 * TOK, TOK), 8 * TOK)
-        gdn[:, part] = dot(hid_hi[...], xbuf[:, part]) + dot(hid_lo[...], xbuf[:, part])
-        exchange(1, gdn, 0, ch)
-
-    scatter(1, gdn, 0)
+    def _(n):
+        for u in range(4):
+            i = 4 * n + u
+            feed = xbuf[:, rows(2 * chip_at(i), 2 * TOK)]
+            gdn[:, rows(2 * i, 2 * TOK)] = dot(hid_hi[...], feed) + dot(hid_lo[...], feed)
+        exchange(1, gdn, 0, n)
+
+        @pl.when(n > 0)
+        def _():
+            forward(n - 1)
+
+    forward(3)
+    rs_r2[1, N // 2 - 1] = rs_s2[1, N // 2 - 1]
     gdown_ref[...] = total(1)
 
     for a in range(3):
@@ -422,12 +451,12 @@
     student_out, grad_down, grad_up = pl.pallas_call(
         kernel,
         out_shape=(
-            jax.ShapeDtypeStruct((TOK, WIDTH), BF16),
-            jax.ShapeDtypeStruct((RANK, HD), F32),
-            jax.ShapeDtypeStruct((RANK, HD), F32),
+            pltpu.VMEM((TOK, WIDTH), BF16),
+            pltpu.VMEM((RANK, HD), F32),
+            pltpu.VMEM((RANK, HD), F32),
         ),
         in_specs=[anywhere] * 6 + [pl.BlockSpec(memory_space=pltpu.SMEM)],
-        out_specs=(anywhere, vmem, vmem),
+        out_specs=(vmem, vmem, vmem),
         scratch_shapes=[
             pltpu.VMEM((TOK, WIDTH), BF16),
             pltpu.VMEM((RANK, WIDTH), BF16),

time: 137 us -> 129 us (0.942)
  Pallas kernels: 132 us -> 126 us
  local copies, waits for them, and re-layouts: 3.68 us -> 2.2 us
    pallas_call x1, Pallas kernels: 132 us -> 126 us  [local(): pl.pallas_call(kernel, out_shape=(pltpu.VMEM((TOK, WIDTH), BF16), pltpu.V...]
    unnamed x7 -> x3, local copies, waits for them, and re-layouts: 3.68 us -> 2.2 us
where the time goes in v3:
time: 129 us
  Pallas kernels  126 us (98%)
  local copies, waits for them, and re-layouts  2.2 us (2%)
    pallas_call x1, Pallas kernels, local(): pl.pallas_call(kernel, out_shape=(pltpu.VMEM((TOK, WIDTH), BF16), pltpu.V...  126 us

profile of v3, /device:TPU:1, one launch (start us, length us, event | category | flops | bytes accessed | tf_op | source)
XLA Modules:
  0.0 129.2 jit_solution(4352965092400194171)
XLA Ops:
  0.6 126.4 %shard_map.94 = (bf16[128,4096]{1,0:T(8,128)(2,1)S(1)}, f32[64,128]{1,0:T(8,128)S(1)}, f32[64,128]{1,0:T(8,128)S(1)}) custom-call(bf16[128,4096]{1,0:T(8,128)(2,1)} %q_hbm.1, bf16[128,4096]{1,0:T(8,128)(2,1)} %k_hbm.1, bf16[128,4096]{1,0:T(8,128)(2,1)} %v_hbm.1, bf16[128,4096]{1,0:T(8,128)(2,1)} %x_hbm.1, bf16[64,4096]{1,0:T(8,128)(2,1)} %bitcast.6, ...), custom_call_target="tpu_custom_call" | custom-call | tf_op jit(solution)/shard_map/pallas_call | solution.py:451
  127.0 1.0 copy.13
  128.0 0.6 copy.14
  128.6 0.6 copy.15

commit v4 on v3

--- a/solution.py
+++ b/solution.py
@@ -222,22 +222,35 @@
     def position(j):
         return lax.rem(z + NZ - ring_step(j), NZ)
 
-    def send_out(j):
-        s = device(lax.rem(j // 2, 2), position(j // 4), lax.rem(j, 2))
-
-        @pl.when(s == me)
-        def _():
-            pltpu.make_async_copy(obuf.at[rows(s)], out_hbm.at[:, cols(me)], osem.at[2]).start()
-
-        @pl.when(s != me)
-        def _():
-            remote(
-                obuf.at[rows(s)], out_hbm.at[:, cols(me)], osem.at[0], osem.at[1], s
-            ).start()
+    def student_slab(j):
+        quad, at = j // 4, lax.rem(j, 4)
+        far, outer, side = (quad + 1) // 2, lax.rem(quad + 1, 2), lax.rem(at, 2)
+        return device(
+            at // 2,
+            lax.rem(z + NZ + (2 * side - 1) * far, NZ),
+            (1 - side) * (1 - outer) + side * outer,
+        )
+
+    def send_out(quad):
+        @pl.loop(4 * quad, 4 * quad + 4)
+        def _(j):
+            s = student_slab(j)
+
+            @pl.when(s == me)
+            def _():
+                pltpu.make_async_copy(
+                    obuf.at[rows(s)], out_hbm.at[:, cols(me)], osem.at[2]
+                ).start()
+
+            @pl.when(s != me)
+            def _():
+                remote(
+                    obuf.at[rows(s)], out_hbm.at[:, cols(me)], osem.at[0], osem.at[1], s
+                ).start()
 
     def done(k):
         f = (k + 1) // 2
-        return (2 * f - 3) * ((f + 2) // 4) + 3 * (k // NZ)
+        return (2 * f - 2) * ((f + 2) // 4) + 2 * (k // NZ)
 
     @pl.loop(0, NZ)
     def _(g):
@@ -259,25 +272,24 @@
 
         @pl.loop(done(g), done(g + 1))
         def _(j):
-            if True:
-                slabs = [device(at // 2, position(j), at % 2) for at in range(4)]
-                seen = [dot(svd[rows(s + 1), HD:], expand[...]) for s in slabs]
-                raw = [dot(qbuf[rows(s), :], keys_t[:, rows(s, 3 * TOK)]) for s in slabs]
-                raw = [jnp.where(m > 0.5, r, -1e30) for m, r in zip(seen, raw)]
-                most = [jnp.max(r, axis=1, keepdims=True) for r in raw]
-                expo = [jnp.exp2((r - m) * EXP2_SCALE) for r, m in zip(raw, most)]
-                norm = [1.0 / jnp.sum(e, axis=1, keepdims=True) for e in expo]
-                weights = [(e * n).astype(BF16) for e, n in zip(expo, norm)]
-                mixed = [dot(w, svd[rows(s, 3 * TOK), :]) for w, s in zip(weights, slabs)]
-                for s, w, m in zip(slabs, weights, mixed):
-                    wts[s] = w
-                    stu[rows(s), :] = m[:, :HD]
-                    obuf[rows(s), :] = m[:, :HD].astype(BF16)
-                    mixd[rows(s), :] = m[:, HD:].astype(BF16)
-
-        @pl.loop(4 * done(g), 4 * done(g + 1))
-        def _(j):
-            send_out(j)
+            slabs = [student_slab(4 * j + at) for at in range(4)]
+            seen = [dot(svd[rows(s + 1), HD:], expand[...]) for s in slabs]
+            raw = [dot(qbuf[rows(s), :], keys_t[:, rows(s, 3 * TOK)]) for s in slabs]
+            raw = [jnp.where(m > 0.5, r, -1e30) for m, r in zip(seen, raw)]
+            most = [jnp.max(r, axis=1, keepdims=True) for r in raw]
+            expo = [jnp.exp2((r - m) * EXP2_SCALE) for r, m in zip(raw, most)]
+            norm = [1.0 / jnp.sum(e, axis=1, keepdims=True) for e in expo]
+            weights = [(e * n).astype(BF16) for e, n in zip(expo, norm)]
+            mixed = [dot(w, svd[rows(s, 3 * TOK), :]) for w, s in zip(weights, slabs)]
+            for s, w, m in zip(slabs, weights, mixed):
+                wts[s] = w
+                stu[rows(s), :] = m[:, :HD]
+                obuf[rows(s), :] = m[:, :HD].astype(BF16)
+                mixd[rows(s), :] = m[:, HD:].astype(BF16)
+
+            @pl.when(j > done(g))
+            def _():
+                send_out(j - 1)
 
         firsts = [(yy * NZ + place) * 2 for yy in range(2)]
 
@@ -315,6 +327,11 @@
 
         blocks = TOKENS // BQ
         score(0, scores0, tops0)
+
+        @pl.when(done(g + 1) > done(g))
+        def _():
+            send_out(done(g + 1) - 1)
+
 
         @pl.loop(0, blocks // 2 - 1)
         def _(i):

time: 129 us -> 127 us (0.984)
  Pallas kernels: 126 us -> 124 us
    pallas_call x1, Pallas kernels: 126 us -> 124 us  [local(): pl.pallas_call(kernel, out_shape=(pltpu.VMEM((TOK, WIDTH), BF16), pltpu.V...]
where the time goes in v4:
time: 127 us
  Pallas kernels  124 us (98%)
  local copies, waits for them, and re-layouts  2.2 us (2%)
    pallas_call x1, Pallas kernels, local(): pl.pallas_call(kernel, out_shape=(pltpu.VMEM((TOK, WIDTH), BF16), pltpu.V...  124 us

profile of v4, /device:TPU:1, one launch (start us, length us, event | category | flops | bytes accessed | tf_op | source)
XLA Modules:
  0.0 126.6 jit_solution(12490455422124476020)
XLA Ops:
  0.6 123.8 %shard_map.94 = (bf16[128,4096]{1,0:T(8,128)(2,1)S(1)}, f32[64,128]{1,0:T(8,128)S(1)}, f32[64,128]{1,0:T(8,128)S(1)}) custom-call(bf16[128,4096]{1,0:T(8,128)(2,1)} %q_hbm.1, bf16[128,4096]{1,0:T(8,128)(2,1)} %k_hbm.1, bf16[128,4096]{1,0:T(8,128)(2,1)} %v_hbm.1, bf16[128,4096]{1,0:T(8,128)(2,1)} %x_hbm.1, bf16[64,4096]{1,0:T(8,128)(2,1)} %bitcast.6, ...), custom_call_target="tpu_custom_call" | custom-call | tf_op jit(solution)/shard_map/pallas_call | solution.py:468
  124.4 1.0 copy.13
  125.4 0.6 copy.14
  126.0 0.6 copy.15

commit v5 on v4

--- a/solution.py
+++ b/solution.py
@@ -185,17 +185,22 @@
         ).start()
 
     def send_all(*arrays):
-        @pl.loop(1, N)
+        @pl.loop(0, N)
         def _(i):
+            far, w = (i + 4) // NZ, lax.rem(i + 4, NZ)
+            side = lax.rem(w, 2)
             target = device(
-                lax.rem(y + lax.rem(i // 2, 2), 2),
-                lax.rem(z + ring_step(i // 4), NZ),
-                lax.rem(c + lax.rem(i, 2), 2),
+                lax.rem(y + lax.rem(w // 2, 2), 2),
+                lax.rem(z + NZ + (1 - 2 * side) * far, NZ),
+                lax.rem(c + w // 4 + side, 2),
             )
-            for hbm, buf, send, sems in arrays:
-                remote(
-                    hbm.at[:, cols(target)], buf.at[rows(me)], send, sems.at[me], target
-                ).start()
+
+            @pl.when(target != me)
+            def _():
+                for hbm, buf, send, sems in arrays:
+                    remote(
+                        hbm.at[:, cols(target)], buf.at[rows(me)], send, sems.at[me], target
+                    ).start()
 
     send_all((q_hbm, qbuf, ssem.at[0], qsem))
 

time: 127 us -> 126 us (level)
  no operation moved by 1% of the time
where the time goes in v5:
time: 126 us
  Pallas kernels  123 us (98%)
  local copies, waits for them, and re-layouts  2.2 us (2%)
    pallas_call x1, Pallas kernels, local(): pl.pallas_call(kernel, out_shape=(pltpu.VMEM((TOK, WIDTH), BF16), pltpu.V...  123 us

profile of v5, /device:TPU:1, one launch (start us, length us, event | category | flops | bytes accessed | tf_op | source)
XLA Modules:
  0.0 126.0 jit_solution(2688899703247126066)
XLA Ops:
  0.6 123.1 %shard_map.94 = (bf16[128,4096]{1,0:T(8,128)(2,1)S(1)}, f32[64,128]{1,0:T(8,128)S(1)}, f32[64,128]{1,0:T(8,128)S(1)}) custom-call(bf16[128,4096]{1,0:T(8,128)(2,1)} %q_hbm.1, bf16[128,4096]{1,0:T(8,128)(2,1)} %k_hbm.1, bf16[128,4096]{1,0:T(8,128)(2,1)} %v_hbm.1, bf16[128,4096]{1,0:T(8,128)(2,1)} %x_hbm.1, bf16[64,4096]{1,0:T(8,128)(2,1)} %bitcast.6, ...), custom_call_target="tpu_custom_call" | custom-call | tf_op jit(solution)/shard_map/pallas_call | solution.py:473
  123.8 1.0 copy.13
  124.7 0.6 copy.14
  125.4 0.6 copy.15
